TPU v7x, 128 devices: a whole 4x4x4 slice. The times are simulated.
128 devices in a mesh: dp: 32 (over x, z, core), rep: 4 (over y).
Axes of the slice: x: 4, y: 4, z: 4, core: 2. Of those that a mesh axis runs over, the one named last changes fastest.
Arguments:
- events: bfloat16 [65536, 512], P(('dp', 'rep')), may hold values from -6 to 6
- grad_out: bfloat16 [65536, 512], P(('dp', 'rep')), may hold values from -15 to 15
- w_uvqk: bfloat16 [512, 2048], replicated, may hold values from -0.25 to 0.25
- w_out: bfloat16 [512, 512], replicated, may hold values from -0.25 to 0.25
- send_place: int32 [128, 512], P(('dp', 'rep')), may hold values from 0 to 1023, as said below
- send_counts: int32 [128, 32], P(('dp', 'rep')), may hold values from 0 to 32, as said below
- user_ids: int32 [128, 512], P(('dp', 'rep')), may hold values from 0 to 15, never falling along the last dimension, each value on 1 to 256 neighbouring positions
Outputs:
- grad_events: bfloat16 [65536, 512], P(('dp', 'rep'))
- grad_w_uvqk: float32 [512, 2048], P(None, 'dp')
- grad_w_out: float32 [512, 512], P(None, 'dp')
Inputs may be any that keep to these rules, and one draw needn't show every extreme that they name: `send_counts`: row d * 4 + r gives, for each owner o of group r, how many events device (d, r) sends there; each row sums to 512, and the counts one owner receives from the 32 devices of its group also sum to 512. `send_place`: an event bound for owner o has place o * 32 + j, where j runs from 0 to that owner's count minus 1 over the device's events bound for o; each place at most once on a device. `user_ids`: each row lists an owner's users in the owner's order of events; ids never fall.
All inputs are finite; a program needn't handle non-finite values.
Results may differ from a plain program's by a relative error of at most 0.02.
Values may be sent and summed in bfloat16 or wider, within the bound.
A program may use at most 192 MiB of HBM per device.

v0:
```python
import jax
import jax.numpy as jnp
from jax import lax
from jax.sharding import PartitionSpec as P

HEADS = 8
EPSILON = 1e-05


def normalized_row_block(values):
    center = values - jnp.mean(values, axis=-1, keepdims=True)
    spread = jnp.mean(center * center, axis=-1, keepdims=True)
    return center * lax.rsqrt(spread + EPSILON)


def hstu_layer(event_row_block, input_weight_matrix, weight_out, allowed):
    width = weight_out.shape[0]
    count = event_row_block.shape[0]
    head_size = width // HEADS
    normalized_input = normalized_row_block(event_row_block.astype(jnp.float32)).astype(
        jnp.bfloat16
    )
    activation_value = jax.nn.silu(
        jnp.dot(normalized_input, input_weight_matrix, preferred_element_type=jnp.float32)
    ).astype(jnp.bfloat16)
    gate_u = activation_value[:, :width]
    values = activation_value[:, width : 2 * width].reshape(count, HEADS, head_size)
    queries = activation_value[:, 2 * width : 3 * width].reshape(count, HEADS, head_size)
    keys = activation_value[:, 3 * width :].reshape(count, HEADS, head_size)
    scores = jnp.einsum(
        "qhd,khd->hqk", queries, keys, preferred_element_type=jnp.float32
    ) * head_size ** (-0.5)
    weights = (jax.nn.silu(scores) * allowed[None]).astype(jnp.bfloat16)
    attended = jnp.einsum(
        "hqk,khd->qhd", weights, values, preferred_element_type=jnp.float32
    ).reshape(count, width)
    gated = (normalized_row_block(attended) * gate_u.astype(jnp.float32)).astype(jnp.bfloat16)
    return event_row_block.astype(jnp.float32) + jnp.dot(
        gated, weight_out, preferred_element_type=jnp.float32
    )


def owner_grads(event_row_block, cotangent, input_weight_matrix, weight_out, allowed):
    result, pullback = jax.vjp(
        lambda first, second, third: hstu_layer(first, second, third, allowed),
        event_row_block,
        input_weight_matrix,
        weight_out,
    )
    return pullback(cotangent.astype(jnp.float32))


def on_device(events, grad_out, w_uvqk, w_out, send_place, send_counts, user_ids):
    owners = lax.axis_size("dp")
    owned = events.shape[0]
    width = events.shape[1]
    capacity = 2 * owned // owners
    places_out = send_place[0]
    send_rows = jnp.zeros((owners * capacity, width), jnp.bfloat16).at[places_out].set(events)
    send_grads = jnp.zeros((owners * capacity, width), jnp.bfloat16).at[places_out].set(grad_out)
    recv_rows, recv_grads = (
        lax.all_to_all(send_rows, "dp", split_axis=0, concat_axis=0, tiled=True),
        lax.all_to_all(send_grads, "dp", split_axis=0, concat_axis=0, tiled=True),
    )
    count_table = lax.all_gather(send_counts, "dp", axis=0, tiled=True)
    own_index = lax.axis_index("dp")
    counts_in = lax.dynamic_slice_in_dim(count_table, own_index, 1, 1)[:, 0]
    users = user_ids[0]
    target_positions = jnp.arange(owners * capacity, dtype=jnp.int32)
    source = target_positions // capacity
    within = target_positions - source * capacity
    starts = jnp.cumsum(counts_in) - counts_in
    onehot = (jnp.arange(owners, dtype=jnp.int32)[None, :] == source[:, None]).astype(jnp.int32)
    count_at = jnp.sum(onehot * counts_in[None, :], axis=1)
    starting_offset = jnp.sum(onehot * starts[None, :], axis=1)
    valid = within < count_at
    position = jnp.minimum(starting_offset + within, owned - 1)
    slot_users = jnp.take(users, position)
    allowed = (
        valid[:, None]
        & valid[None, :]
        & (slot_users[:, None] == slot_users[None, :])
        & (target_positions[None, :] <= target_positions[:, None])
    ).astype(jnp.float32)
    grad_rows, grad_in, grad_outw = owner_grads(recv_rows, recv_grads, w_uvqk, w_out, allowed)
    returned = lax.all_to_all(grad_rows, "dp", split_axis=0, concat_axis=0, tiled=True)
    grad_events = jnp.take(returned, places_out, axis=0)
    grad_in = grad_in.astype(jnp.float32)
    grad_outw = grad_outw.astype(jnp.float32)
    part_in, part_out = (
        lax.psum_scatter(
            grad_in.astype(jnp.bfloat16), "dp", scatter_dimension=1, tiled=True
        ).astype(jnp.float32),
        lax.psum_scatter(
            grad_outw.astype(jnp.bfloat16), "dp", scatter_dimension=1, tiled=True
        ).astype(jnp.float32),
    )
    share_in, share_out = (
        lax.psum(part_in.astype(jnp.bfloat16), "rep").astype(jnp.float32),
        lax.psum(part_out.astype(jnp.bfloat16), "rep").astype(jnp.float32),
    )
    return (grad_events, share_in, share_out)


def solution(mesh):
    return jax.shard_map(
        on_device,
        mesh=mesh,
        in_specs=(
            P(("dp", "rep"), None),
            P(("dp", "rep"), None),
            P(),
            P(),
            P(("dp", "rep"), None),
            P(("dp", "rep"), None),
            P(("dp", "rep"), None),
        ),
        out_specs=(P(("dp", "rep"), None), P(None, "dp"), P(None, "dp")),
        check_vma=False,
    )
```

profile of v0, /device:TPU:0, one launch (start us, length us, event | category | flops | bytes accessed | tf_op | source)
XLA Modules:
  0.0 388.2 jit_solution(12523036387752850072)
XLA Ops:
  8.0 4.0 %scatter_custom_fusion.1 = bf16[1024,512]{1,0:T(8,128)(2,1)} fusion(s32[512]{0:T(512)S(1)} %bitcast.106, bf16[512,512]{1,0:T(8,128)(2,1)} %param.7, bf16[]{:T(256)} %constant.83.clone.1), kind=kCustom, calls=%fused_computation.50 | custom fusion | bytes 1049088 | tf_op jit(solution)/shard_map/scatter | solution.py:59
  12.0 8.3 %all-to-all-start.1 = ((bf16[32,32,512]{2,1,0:T(8,128)(2,1)}), bf16[32,32,512]{2,1,0:T(8,128)(2,1)S(1)}, u32[]{:S(2)}, u32[]{:S(2)}) async-start(bf16[32,32,512]{2,1,0:T(8,128)(2,1)} %bitcast.95), calls=%async_computation.1 | async-start | bytes 2097152 | tf_op jit(solution)/shard_map/all_to_all | solution.py:62
  20.3 29.8 %all-gather = s32[32,1,32]{2,1,0:T(1,128)S(1)} all-gather(s32[1,1,32]{2,1,0:T(1,128)} %bitcast.110), channel_id=1, replica_groups=mesh['dp'=32,'rep'=4] {'dp'}, dimensions={0}, use_global_device_ids=true | all-gather | bytes 4224 | tf_op jit(solution)/shard_map/all_gather | solution.py:65
  51.1 4.0 %scatter_custom_fusion = bf16[1024,512]{1,0:T(8,128)(2,1)} fusion(s32[512]{0:T(512)S(1)} %bitcast.107, bf16[512,512]{1,0:T(8,128)(2,1)} %param.8, bf16[]{:T(256)} %constant.83.clone.1), kind=kCustom, calls=%fused_computation.52 | custom fusion | bytes 1049088 | tf_op jit(solution)/shard_map/scatter | solution.py:60
  55.1 6.9 %gather_fusion = s32[1024]{0:T(1024)S(1)} fusion(s32[512]{0:T(512)S(1)} %bitcast.87, s32[1024]{0:T(1024)S(1)} %broadcast_clamp_fusion), kind=kCustom, calls=%fused_computation | custom fusion | bytes 12288 | tf_op jit(solution)/shard_map/jit(_take)/gather | solution.py:78
  62.0 2.9 fusion.6
  65.0 6.0 %all-to-all-start = ((bf16[32,32,512]{2,1,0:T(8,128)(2,1)}), bf16[32,32,512]{2,1,0:T(8,128)(2,1)}, u32[]{:S(2)}, u32[]{:S(2)}) async-start(bf16[32,32,512]{2,1,0:T(8,128)(2,1)} %bitcast.96), calls=%async_computation | async-start | bytes 2097152 | tf_op jit(solution)/shard_map/all_to_all | solution.py:63
  72.6 5.7 %multiply_convert_fusion.1 = (bf16[1024,2048]{0,1:T(8,128)(2,1)S(1)}, f32[1024,2048]{0,1:T(8,128)}) fusion(bf16[1024,512]{1,0:T(8,128)(2,1)S(1)} %multiply_convert_fusion.2, bf16[512,2048]{1,0:T(8,128)(2,1)S(1)} %copy-done), kind=kOutput, calls=%fused_computation.15 | convolution fusion | flops 2157969408 | bytes 15728640 | tf_op jit(solution)/shard_map/jvp()/dot_general | solution.py:24
  78.3 1.9 copy-done.5
  82.0 21.5 %multiply_convert_fusion = (bf16[8,1024,1024]{2,1,0:T(8,128)(2,1)}, f32[8,1024,1024]{2,1,0:T(8,128)}) fusion(f32[1024,1024]{1,0:T(8,128)} %fusion.6, bf16[1024,8,64]{0,2,1:T(8,128)(2,1)S(1)} %bitcast.90, bf16[1024,8,64]{0,2,1:T(8,128)(2,1)} %bitcast.101), kind=kOutput, calls=%fused_computation.8 | convolution fusion | flops 1132462080 | bytes 56623104 | tf_op jit(solution)/shard_map/jvp(qhd,khd->hqk)/dot_general | solution.py:30
  103.5 12.7 %fusion.29 = (f32[1024]{0:T(1024)S(1)}, f32[8,64,1024]{2,1,0:T(8,128)}) fusion(bf16[1024,8,64]{0,2,1:T(8,128)(2,1)} %bitcast.98, bf16[8,1024,1024]{2,1,0:T(8,128)(2,1)} %get-tuple-element.17), kind=kOutput, calls=%fused_computation.96 | convolution fusion | flops 1074265088 | bytes 19927040 | tf_op jit(solution)/shard_map/jvp(hqk,khd->qhd)/dot_general | solution.py:34
  116.1 1.8 fusion.11
  118.0 3.2 multiply_reduce_fusion
  121.2 4.4 %fusion.8 = (bf16[1024,512]{0,1:T(8,128)(2,1)S(1)}, f32[1024]{0:T(1024)S(1)}, bf16[1024,512]{0,1:T(8,128)(2,1)}) fusion(f32[8,64,1024]{2,1,0:T(8,128)} %get-tuple-element.20, f32[1024]{0:T(1024)S(1)} %broadcast_multiply_fusion.1, f32[1024]{0:T(1024)S(1)} %get-tuple-element.14, bf16[1024,2048]{0,1:T(8,128)(2,1)} %copy-done.5, f32[1024]{0:T(1024)S(1)} %get-tuple-element.13, ...), kind=kLoop, calls=%fused_computation.29 | loop fusion | flops 7339008 | bytes 6307840 | tf_op jit(solution)/shard_map/jvp()/convert_element_type | solution.py:37
  125.6 2.6 broadcast_add_fusion
  128.2 4.0 %fusion.33 = bf16[8,64,1024]{2,1,0:T(8,128)(2,1)} fusion(bf16[8,64,1024]{2,1,0:T(8,128)(2,1)S(1)} %bitcast.93, bf16[8,1024,1024]{2,1,0:T(8,128)(2,1)S(1)} %copy-done.2), kind=kOutput, calls=%fused_computation.100 | convolution fusion | flops 1073741824 | bytes 18874368 | tf_op jit(solution)/shard_map/transpose(jvp(hqk,khd->qhd))/dot_general | solution.py:34
  132.2 23.7 %fusion.2 = bf16[8,1024,1024]{2,1,0:T(8,128)(2,1)} fusion(f32[8,1024,1024]{2,1,0:T(8,128)} %get-tuple-element.18, f32[1024,1024]{1,0:T(8,128)S(1)} %copy-done.8, bf16[8,64,1024]{2,1,0:T(8,128)(2,1)S(1)} %bitcast.94, bf16[1024,8,64]{0,2,1:T(8,128)(2,1)S(1)} %bitcast.99), kind=kOutput, calls=%fused_computation.7 | convolution fusion | flops 1191182336 | bytes 56623104 | tf_op jit(solution)/shard_map/transpose(jvp(hqk,khd->qhd))/dot_general | solution.py:34
  155.9 9.8 %fusion.31 = bf16[8,1024,64]{1,2,0:T(8,128)(2,1)} fusion(bf16[8,1024,1024]{2,1,0:T(8,128)(2,1)} %fusion.2, bf16[1024,8,64]{0,2,1:T(8,128)(2,1)S(1)} %bitcast.102), kind=kOutput, calls=%fused_computation.98 | convolution fusion | flops 1073741824 | bytes 18874368 | tf_op jit(solution)/shard_map/transpose(jvp(qhd,khd->hqk))/dot_general | solution.py:30
  165.8 7.5 %fusion.32 = bf16[8,1024,64]{1,2,0:T(8,128)(2,1)S(1)} fusion(bf16[8,1024,1024]{2,1,0:T(8,128)(2,1)} %fusion.2, bf16[1024,8,64]{0,2,1:T(8,128)(2,1)S(1)} %bitcast.91), kind=kOutput, calls=%fused_computation.99 | convolution fusion | flops 1073741824 | bytes 18874368 | tf_op jit(solution)/shard_map/transpose(jvp(qhd,khd->hqk))/dot_general | solution.py:30
  173.2 2.8 convolution_convert_fusion.6
  176.1 6.4 %fusion.3 = bf16[1024,2048]{0,1:T(8,128)(2,1)S(1)} fusion(f32[1024,2048]{0,1:T(8,128)} %get-tuple-element.16, bf16[1024,512]{0,1:T(8,128)(2,1)} %get-tuple-element.12, bf16[1024,512]{0,1:T(8,128)(2,1)} %bitcast.92, bf16[1024,512]{0,1:T(8,128)(2,1)} %bitcast.100, bf16[1024,512]{0,1:T(8,128)(2,1)S(1)} %bitcast.89), kind=kLoop, calls=%fused_computation.13 | loop fusion | flops 37748736 | bytes 16777216 | tf_op jit(solution)/shard_map/transpose(jvp(jit(silu)))/add_any | solution.py:23
  182.5 1.9 copy-done.9
  184.4 3.7 fusion.30
  188.2 4.9 %fusion.9 = (f32[1024]{0:T(1024)S(1)}, bf16[1024,512]{1,0:T(8,128)(2,1)S(1)}) fusion(bf16[32,32,512]{2,1,0:T(8,128)(2,1)S(1)} %copy-done.4, f32[1024]{0:T(1024)S(1)} %copy-done.16, bf16[1024,2048]{0,1:T(8,128)(2,1)} %copy-done.9, bf16[512,2048]{1,0:T(8,128)(2,1)S(1)} %copy-done), kind=kOutput, calls=%fused_computation.30 | convolution fusion | flops 2150104064 | bytes 8396800 | tf_op jit(solution)/shard_map/transpose(jvp())/dot_general | solution.py:24
  194.2 2.8 fusion.13
  197.0 7.3 %all-to-all-start.2 = ((bf16[32,32,512]{2,1,0:T(8,128)(2,1)}), bf16[32,32,512]{2,1,0:T(8,128)(2,1)S(1)}, u32[]{:S(2)}, u32[]{:S(2)}) async-start(bf16[32,32,512]{2,1,0:T(8,128)(2,1)} %bitcast.97), calls=%async_computation.2 | async-start | bytes 2097152 | tf_op jit(solution)/shard_map/all_to_all | solution.py:86
  204.4 50.9 %reduce-scatter.5.cloned.1.call-done = bf16[512,16]{0,1:T(8,128)(2,1)} async-done(((bf16[512,512]{0,1:T(8,128)(2,1)}), bf16[512,16]{0,1:T(8,128)(2,1)}) %reduce-scatter.5.cloned.1.call-update) | async-done | bytes 16400 | tf_op jit(solution)/shard_map/reduce_scatter | solution.py:94
  255.3 17.5 %psum.15 = bf16[512,16]{0,1:T(8,128)(2,1)S(1)} all-reduce(bf16[512,16]{0,1:T(8,128)(2,1)} %reduce-scatter.5.cloned.1.call-done), channel_id=1, replica_groups=mesh['dp'=32,'rep'=4] {'rep'}, use_global_device_ids=true, to_apply=%region_16.17 | all-reduce | flops 8192 | bytes 32768 | tf_op jit(solution)/shard_map/psum | solution.py:100
  273.4 2.6 gather_fusion.1
  276.0 61.1 %reduce-scatter.3.cloned.1.call-done = bf16[512,64]{0,1:T(8,128)(2,1)} async-done(((bf16[512,2048]{0,1:T(8,128)(2,1)}), bf16[512,64]{0,1:T(8,128)(2,1)}) %reduce-scatter.3.cloned.1.call-update) | async-done | bytes 65552 | tf_op jit(solution)/shard_map/reduce_scatter | solution.py:91
  337.2 2.0 broadcast_select_fusion
  339.2 40.8 %all-reduce.6.cloned.1.call-done = bf16[512,64]{0,1:T(8,128)(2,1)} async-done(((bf16[512,64]{0,1:T(8,128)(2,1)}), bf16[512,64]{0,1:T(8,128)(2,1)}) %all-reduce.6.cloned.1.call-update) | async-done | bytes 65552 | tf_op jit(solution)/shard_map/psum | solution.py:99
  (85 shorter events, 8.6 us)
Async XLA Ops:
  7.2 65.4 %copy-start = (bf16[512,2048]{1,0:T(8,128)(2,1)S(1)}, bf16[512,2048]{1,0:T(8,128)(2,1)}, u32[]{:S(2)}) copy-start(bf16[512,2048]{1,0:T(8,128)(2,1)} %param.9) | copy-start | bytes 6291460
  7.2 47.9 %copy-start.1 = (s32[1,512]{1,0:T(1,128)S(1)}, s32[1,512]{1,0:T(1,128)}, u32[]{:S(2)}) copy-start(s32[1,512]{1,0:T(1,128)} %param.13) | copy-start | bytes 6148
  8.0 54.0 %copy-start.21 = (s32[512,1]{0,1:T(1,128)}, s32[512,1]{0,1:T(1,128)S(1)}, u32[]{:S(2)}) copy-start(s32[512,1]{0,1:T(1,128)S(1)} %compare_select_fusion.1) | copy-start | bytes 6148
  12.0 53.0 %all-to-all-start.1 = ((bf16[32,32,512]{2,1,0:T(8,128)(2,1)}), bf16[32,32,512]{2,1,0:T(8,128)(2,1)S(1)}, u32[]{:S(2)}, u32[]{:S(2)}) async-start(bf16[32,32,512]{2,1,0:T(8,128)(2,1)} %bitcast.95), calls=%async_computation.1 | async-start | bytes 2097152 | tf_op jit(solution)/shard_map/all_to_all | solution.py:62
  65.0 13.3 %copy-start.3 = (bf16[32,32,512]{2,1,0:T(8,128)(2,1)}, bf16[32,32,512]{2,1,0:T(8,128)(2,1)S(1)}, u32[]{:S(2)}) copy-start(bf16[32,32,512]{2,1,0:T(8,128)(2,1)S(1)} %all-to-all-done.1) | copy-start | bytes 3145732
  65.0 53.0 %all-to-all-start = ((bf16[32,32,512]{2,1,0:T(8,128)(2,1)}), bf16[32,32,512]{2,1,0:T(8,128)(2,1)}, u32[]{:S(2)}, u32[]{:S(2)}) async-start(bf16[32,32,512]{2,1,0:T(8,128)(2,1)} %bitcast.96), calls=%async_computation | async-start | bytes 2097152 | tf_op jit(solution)/shard_map/all_to_all | solution.py:63
  70.9 184.3 %reduce-scatter.5.cloned.1.call-start = ((), (), s32[]{:S(2)}) async-start(), calls=%async_computation.7 | async-start | bytes 540672 | tf_op jit(solution)/shard_map/reduce_scatter | solution.py:94
  71.6 6.7 %copy-start.15 = (f32[1024]{0:T(1024)}, f32[1024]{0:T(1024)S(1)}, u32[]{:S(2)}) copy-start(f32[1024]{0:T(1024)S(1)} %div.65) | copy-start | bytes 12292
  72.2 6.1 %copy-start.19 = (f32[1024]{0:T(1024)}, f32[1024]{0:T(1024)S(1)}, u32[]{:S(2)}) copy-start(f32[1024]{0:T(1024)S(1)} %add.153) | copy-start | bytes 12292
  72.2 6.1 %copy-start.17 = (f32[1024]{0:T(1024)}, f32[1024]{0:T(1024)S(1)}, u32[]{:S(2)}) copy-start(f32[1024]{0:T(1024)S(1)} %rsqrt.20) | copy-start | bytes 12292
  72.6 5.7 %copy-start.11 = (bf16[1024,512]{1,0:T(8,128)(2,1)}, bf16[1024,512]{1,0:T(8,128)(2,1)S(1)}, u32[]{:S(2)}) copy-start(bf16[1024,512]{1,0:T(8,128)(2,1)S(1)} %multiply_convert_fusion.2) | copy-start | bytes 3145732
  78.3 1.9 copy-start.5
  82.0 21.5 %copy-start.6 = (bf16[1024,512]{0,1:T(8,128)(2,1)}, bf16[1024,512]{0,1:T(8,128)(2,1)S(1)}, u32[]{:S(2)}) copy-start(bf16[1024,512]{0,1:T(8,128)(2,1)S(1)} %get-tuple-element.10) | copy-start | bytes 3145732
  103.5 14.5 %copy-start.14 = (bf16[512,512]{1,0:T(8,128)(2,1)S(1)}, bf16[512,512]{1,0:T(8,128)(2,1)}, u32[]{:S(2)}) copy-start(bf16[512,512]{1,0:T(8,128)(2,1)} %param.10) | copy-start | bytes 1572868
  118.0 10.1 %copy-start.2 = (bf16[8,1024,1024]{2,1,0:T(8,128)(2,1)S(1)}, bf16[8,1024,1024]{2,1,0:T(8,128)(2,1)}, u32[]{:S(2)}) copy-start(bf16[8,1024,1024]{2,1,0:T(8,128)(2,1)} %get-tuple-element.17) | copy-start | bytes 50331652
  128.1 4.0 %copy-start.8 = (f32[1024,1024]{1,0:T(8,128)S(1)}, f32[1024,1024]{1,0:T(8,128)}, u32[]{:S(2)}) copy-start(f32[1024,1024]{1,0:T(8,128)} %fusion.6) | copy-start | bytes 12582916
  128.2 4.0 %copy-start.10 = (bf16[1024,512]{0,1:T(8,128)(2,1)S(1)}, bf16[1024,512]{0,1:T(8,128)(2,1)}, u32[]{:S(2)}) copy-start(bf16[1024,512]{0,1:T(8,128)(2,1)} %get-tuple-element.11) | copy-start | bytes 3145732
  132.2 23.7 %copy-start.13 = (bf16[1024,512]{0,1:T(8,128)(2,1)S(1)}, bf16[1024,512]{0,1:T(8,128)(2,1)}, u32[]{:S(2)}) copy-start(bf16[1024,512]{0,1:T(8,128)(2,1)} %get-tuple-element.9) | copy-start | bytes 3145732
  155.9 9.9 %copy-start.7 = (bf16[1024,512]{0,1:T(8,128)(2,1)S(1)}, bf16[1024,512]{0,1:T(8,128)(2,1)}, u32[]{:S(2)}) copy-start(bf16[1024,512]{0,1:T(8,128)(2,1)} %copy-done.6) | copy-start | bytes 3145732
  176.1 161.1 %reduce-scatter.3.cloned.1.call-start = ((), (), s32[]{:S(2)}) async-start(), calls=%async_computation.5 | async-start | bytes 2162688 | tf_op jit(solution)/shard_map/reduce_scatter | solution.py:91
  176.1 8.3 %copy-start.12 = (bf16[1024,512]{1,0:T(8,128)(2,1)S(1)}, bf16[1024,512]{1,0:T(8,128)(2,1)}, u32[]{:S(2)}) copy-start(bf16[1024,512]{1,0:T(8,128)(2,1)} %copy-done.11) | copy-start | bytes 3145732
  182.5 1.9 copy-start.9
  184.4 3.7 copy-start.4
  184.4 3.7 copy-start.16
  188.2 4.9 %copy-start.20 = (f32[1024]{0:T(1024)S(1)}, f32[1024]{0:T(1024)}, u32[]{:S(2)}) copy-start(f32[1024]{0:T(1024)} %copy-done.19) | copy-start | bytes 12292
  188.2 4.9 %copy-start.18 = (f32[1024]{0:T(1024)S(1)}, f32[1024]{0:T(1024)}, u32[]{:S(2)}) copy-start(f32[1024]{0:T(1024)} %copy-done.17) | copy-start | bytes 12292
  193.1 11.3 %copy-start.22 = (s32[512,1]{0,1:T(1,128)S(1)}, s32[512,1]{0,1:T(1,128)}, u32[]{:S(2)}) copy-start(s32[512,1]{0,1:T(1,128)} %copy-done.21) | copy-start | bytes 6148
  193.1 11.3 %copy-start.23 = (s32[1,512]{1,0:T(1,128)S(1)}, s32[1,512]{1,0:T(1,128)}, u32[]{:S(2)}) copy-start(s32[1,512]{1,0:T(1,128)} %param.11) | copy-start | bytes 6148
  197.0 76.4 %all-to-all-start.2 = ((bf16[32,32,512]{2,1,0:T(8,128)(2,1)}), bf16[32,32,512]{2,1,0:T(8,128)(2,1)S(1)}, u32[]{:S(2)}, u32[]{:S(2)}) async-start(bf16[32,32,512]{2,1,0:T(8,128)(2,1)} %bitcast.97), calls=%async_computation.2 | async-start | bytes 2097152 | tf_op jit(solution)/shard_map/all_to_all | solution.py:86
  204.3 175.6 %all-reduce.6.cloned.1.call-start = ((), (), s32[]{:S(2)}) async-start(), calls=%async_computation.6 | async-start | bytes 131072 | tf_op jit(solution)/shard_map/psum | solution.py:99
Sparse Core Ops, SparseCore 0:
  176.2 79.0 reduce-scatter.4
  258.8 78.2 reduce-scatter.2
  339.5 40.4 all-reduce.5
where the time goes:
time: 395 us; the launch traced here: 388 us
  waiting for transfers between devices  153 us (39%)
  matrix products  99.4 us (25%)
  blocking collectives  47.3 us (12%)
  other arithmetic  28.3 us (7%)
  local copies, waits for them, and re-layouts  24 us (6%)
  starting transfers between devices  22 us (6%)
  between operations  14.4 us (4%)
    reduce_scatter x1, waiting for transfers between devices, on_device(): lax.psum_scatter(grad_in.astype(jnp.bfloat16), 'dp', scatter_dimension=1,...  61.1 us
    reduce_scatter x1, waiting for transfers between devices, on_device(): lax.psum_scatter(grad_outw.astype(jnp.bfloat16), 'dp', scatter_dimension=...  50.9 us
    psum x1, waiting for transfers between devices, on_device(): lax.psum(part_in.astype(jnp.bfloat16), 'rep').astype(jnp.float32)  40.8 us
    dot_general x3, matrix products, hstu_layer(): jnp.einsum('hqk,khd->qhd', weights, values, preferred_element_type=jnp.fl...  40.4 us
    dot_general x3, matrix products, hstu_layer(): jnp.einsum('qhd,khd->hqk', queries, keys, preferred_element_type=jnp.floa...  38.8 us
    all_gather x1, blocking collectives, on_device(): count_table = lax.all_gather(send_counts, 'dp', axis=0, tiled=True)  29.8 us
    psum x1, blocking collectives, on_device(): lax.psum(part_out.astype(jnp.bfloat16), 'rep').astype(jnp.float32)  17.5 us
    dot_general x3, matrix products, hstu_layer(): jnp.dot(normalized_input, input_weight_matrix, preferred_element_type=jnp...  14.3 us
  transfers between devices with their start and end apart: 6, of which 3 were waited for; matrix products, arithmetic and copies ran while one was open for 22% of the time, Pallas kernels for 0%

commit v1 on v0

--- a/solution.py
+++ b/solution.py
@@ -96,7 +96,7 @@
         ).astype(jnp.float32),
     )
     share_in, share_out = (
-        lax.psum(part_in.astype(jnp.bfloat16), "rep").astype(jnp.float32),
+        jnp.sum(lax.all_gather(part_in.astype(jnp.bfloat16), "rep"), axis=0).astype(jnp.float32),
         lax.psum(part_out.astype(jnp.bfloat16), "rep").astype(jnp.float32),
     )
     return (grad_events, share_in, share_out)

time: 395 us -> 365 us (0.924)
  waiting for transfers between devices: 153 us -> 110 us
  blocking collectives: 47.3 us -> 60.1 us
    psum x1 -> x0, waiting for transfers between devices: 40.8 us -> none  [on_device(): lax.psum(part_in.astype(jnp.bfloat16), 'rep').astype(jnp.float32)]
    all_gather x0 -> x1, blocking collectives: none -> 12.9 us  [on_device(): lax.all_gather(part_in.astype(jnp.bfloat16), 'rep')]
  transfers between devices with their start and end apart: 6 -> 5, of which waited for: 3 -> 2; matrix products, arithmetic and copies ran while one was open for 22% -> 23% of each run, Pallas kernels for 0% -> 0%
where the time goes in v1:
time: 365 us; the launch traced here: 358 us
  waiting for transfers between devices  110 us (30%)
  matrix products  99.4 us (27%)
  blocking collectives  60.1 us (16%)
  other arithmetic  27.8 us (8%)
  local copies, waits for them, and re-layouts  24.2 us (7%)
  starting transfers between devices  21.9 us (6%)
  between operations  14.7 us (4%)
    reduce_scatter x1, waiting for transfers between devices, on_device(): lax.psum_scatter(grad_in.astype(jnp.bfloat16), 'dp', scatter_dimension=1,...  59.2 us
    reduce_scatter x1, waiting for transfers between devices, on_device(): lax.psum_scatter(grad_outw.astype(jnp.bfloat16), 'dp', scatter_dimension=...  50.9 us
    dot_general x3, matrix products, hstu_layer(): jnp.einsum('hqk,khd->qhd', weights, values, preferred_element_type=jnp.fl...  40.4 us
    dot_general x3, matrix products, hstu_layer(): jnp.einsum('qhd,khd->hqk', queries, keys, preferred_element_type=jnp.floa...  38.8 us
    all_gather x1, blocking collectives, on_device(): count_table = lax.all_gather(send_counts, 'dp', axis=0, tiled=True)  29.8 us
    psum x1, blocking collectives, on_device(): lax.psum(part_out.astype(jnp.bfloat16), 'rep').astype(jnp.float32)  17.5 us
    dot_general x3, matrix products, hstu_layer(): jnp.dot(normalized_input, input_weight_matrix, preferred_element_type=jnp...  14.3 us
    all_gather x1, blocking collectives, on_device(): lax.all_gather(part_in.astype(jnp.bfloat16), 'rep')  12.9 us
  transfers between devices with their start and end apart: 5, of which 2 were waited for; matrix products, arithmetic and copies ran while one was open for 23% of the time, Pallas kernels for 0%

profile of v1, /device:TPU:0, one launch (start us, length us, event | category | flops | bytes accessed | tf_op | source)
XLA Modules:
  0.0 358.3 jit_solution(13566527694663402966)
XLA Ops:
  8.0 4.0 %scatter_custom_fusion.1 = bf16[1024,512]{1,0:T(8,128)(2,1)} fusion(s32[512]{0:T(512)S(1)} %bitcast.108, bf16[512,512]{1,0:T(8,128)(2,1)} %param.7, bf16[]{:T(256)} %constant.84.clone.1), kind=kCustom, calls=%fused_computation.50 | custom fusion | bytes 1049088 | tf_op jit(solution)/shard_map/scatter | solution.py:59
  12.0 8.3 %all-to-all-start.1 = ((bf16[32,32,512]{2,1,0:T(8,128)(2,1)}), bf16[32,32,512]{2,1,0:T(8,128)(2,1)S(1)}, u32[]{:S(2)}, u32[]{:S(2)}) async-start(bf16[32,32,512]{2,1,0:T(8,128)(2,1)} %bitcast.97), calls=%async_computation.1 | async-start | bytes 2097152 | tf_op jit(solution)/shard_map/all_to_all | solution.py:62
  20.3 29.8 %all-gather.1 = s32[32,1,32]{2,1,0:T(1,128)S(1)} all-gather(s32[1,1,32]{2,1,0:T(1,128)} %bitcast.112), channel_id=1, replica_groups=mesh['dp'=32,'rep'=4] {'dp'}, dimensions={0}, use_global_device_ids=true | all-gather | bytes 4224 | tf_op jit(solution)/shard_map/all_gather | solution.py:65
  51.1 4.0 %scatter_custom_fusion = bf16[1024,512]{1,0:T(8,128)(2,1)} fusion(s32[512]{0:T(512)S(1)} %bitcast.109, bf16[512,512]{1,0:T(8,128)(2,1)} %param.8, bf16[]{:T(256)} %constant.84.clone.1), kind=kCustom, calls=%fused_computation.52 | custom fusion | bytes 1049088 | tf_op jit(solution)/shard_map/scatter | solution.py:60
  55.1 6.9 %gather_fusion = s32[1024]{0:T(1024)S(1)} fusion(s32[512]{0:T(512)S(1)} %bitcast.89, s32[1024]{0:T(1024)S(1)} %broadcast_clamp_fusion), kind=kCustom, calls=%fused_computation | custom fusion | bytes 12288 | tf_op jit(solution)/shard_map/jit(_take)/gather | solution.py:78
  62.0 2.9 fusion.6
  65.0 6.0 %all-to-all-start = ((bf16[32,32,512]{2,1,0:T(8,128)(2,1)}), bf16[32,32,512]{2,1,0:T(8,128)(2,1)}, u32[]{:S(2)}, u32[]{:S(2)}) async-start(bf16[32,32,512]{2,1,0:T(8,128)(2,1)} %bitcast.98), calls=%async_computation | async-start | bytes 2097152 | tf_op jit(solution)/shard_map/all_to_all | solution.py:63
  72.6 5.7 %multiply_convert_fusion.1 = (bf16[1024,2048]{0,1:T(8,128)(2,1)S(1)}, f32[1024,2048]{0,1:T(8,128)}) fusion(bf16[1024,512]{1,0:T(8,128)(2,1)S(1)} %multiply_convert_fusion.2, bf16[512,2048]{1,0:T(8,128)(2,1)S(1)} %copy-done), kind=kOutput, calls=%fused_computation.15 | convolution fusion | flops 2157969408 | bytes 15728640 | tf_op jit(solution)/shard_map/jvp()/dot_general | solution.py:24
  78.3 1.9 copy-done.5
  82.0 21.5 %multiply_convert_fusion = (bf16[8,1024,1024]{2,1,0:T(8,128)(2,1)}, f32[8,1024,1024]{2,1,0:T(8,128)}) fusion(f32[1024,1024]{1,0:T(8,128)} %fusion.6, bf16[1024,8,64]{0,2,1:T(8,128)(2,1)S(1)} %bitcast.92, bf16[1024,8,64]{0,2,1:T(8,128)(2,1)} %bitcast.103), kind=kOutput, calls=%fused_computation.8 | convolution fusion | flops 1132462080 | bytes 56623104 | tf_op jit(solution)/shard_map/jvp(qhd,khd->hqk)/dot_general | solution.py:30
  103.5 12.7 %fusion.29 = (f32[1024]{0:T(1024)S(1)}, f32[8,64,1024]{2,1,0:T(8,128)}) fusion(bf16[1024,8,64]{0,2,1:T(8,128)(2,1)} %bitcast.100, bf16[8,1024,1024]{2,1,0:T(8,128)(2,1)} %get-tuple-element.17), kind=kOutput, calls=%fused_computation.96 | convolution fusion | flops 1074265088 | bytes 19927040 | tf_op jit(solution)/shard_map/jvp(hqk,khd->qhd)/dot_general | solution.py:34
  116.1 1.8 fusion.11
  118.0 3.2 multiply_reduce_fusion
  121.2 4.4 %fusion.8 = (bf16[1024,512]{0,1:T(8,128)(2,1)S(1)}, f32[1024]{0:T(1024)S(1)}, bf16[1024,512]{0,1:T(8,128)(2,1)}) fusion(f32[8,64,1024]{2,1,0:T(8,128)} %get-tuple-element.20, f32[1024]{0:T(1024)S(1)} %broadcast_multiply_fusion.1, f32[1024]{0:T(1024)S(1)} %get-tuple-element.14, bf16[1024,2048]{0,1:T(8,128)(2,1)} %copy-done.5, f32[1024]{0:T(1024)S(1)} %get-tuple-element.13, ...), kind=kLoop, calls=%fused_computation.29 | loop fusion | flops 7339008 | bytes 6307840 | tf_op jit(solution)/shard_map/jvp()/convert_element_type | solution.py:37
  125.6 2.6 broadcast_add_fusion
  128.2 4.0 %fusion.33 = bf16[8,64,1024]{2,1,0:T(8,128)(2,1)} fusion(bf16[8,64,1024]{2,1,0:T(8,128)(2,1)S(1)} %bitcast.95, bf16[8,1024,1024]{2,1,0:T(8,128)(2,1)S(1)} %copy-done.2), kind=kOutput, calls=%fused_computation.100 | convolution fusion | flops 1073741824 | bytes 18874368 | tf_op jit(solution)/shard_map/transpose(jvp(hqk,khd->qhd))/dot_general | solution.py:34
  132.2 23.7 %fusion.2 = bf16[8,1024,1024]{2,1,0:T(8,128)(2,1)} fusion(f32[8,1024,1024]{2,1,0:T(8,128)} %get-tuple-element.18, f32[1024,1024]{1,0:T(8,128)S(1)} %copy-done.8, bf16[8,64,1024]{2,1,0:T(8,128)(2,1)S(1)} %bitcast.96, bf16[1024,8,64]{0,2,1:T(8,128)(2,1)S(1)} %bitcast.101), kind=kOutput, calls=%fused_computation.7 | convolution fusion | flops 1191182336 | bytes 56623104 | tf_op jit(solution)/shard_map/transpose(jvp(hqk,khd->qhd))/dot_general | solution.py:34
  155.9 9.8 %fusion.31 = bf16[8,1024,64]{1,2,0:T(8,128)(2,1)} fusion(bf16[8,1024,1024]{2,1,0:T(8,128)(2,1)} %fusion.2, bf16[1024,8,64]{0,2,1:T(8,128)(2,1)S(1)} %bitcast.104), kind=kOutput, calls=%fused_computation.98 | convolution fusion | flops 1073741824 | bytes 18874368 | tf_op jit(solution)/shard_map/transpose(jvp(qhd,khd->hqk))/dot_general | solution.py:30
  165.8 7.5 %fusion.32 = bf16[8,1024,64]{1,2,0:T(8,128)(2,1)S(1)} fusion(bf16[8,1024,1024]{2,1,0:T(8,128)(2,1)} %fusion.2, bf16[1024,8,64]{0,2,1:T(8,128)(2,1)S(1)} %bitcast.93), kind=kOutput, calls=%fused_computation.99 | convolution fusion | flops 1073741824 | bytes 18874368 | tf_op jit(solution)/shard_map/transpose(jvp(qhd,khd->hqk))/dot_general | solution.py:30
  173.2 2.8 convolution_convert_fusion.6
  176.1 6.4 %fusion.3 = bf16[1024,2048]{0,1:T(8,128)(2,1)S(1)} fusion(f32[1024,2048]{0,1:T(8,128)} %get-tuple-element.16, bf16[1024,512]{0,1:T(8,128)(2,1)} %get-tuple-element.12, bf16[1024,512]{0,1:T(8,128)(2,1)} %bitcast.94, bf16[1024,512]{0,1:T(8,128)(2,1)} %bitcast.102, bf16[1024,512]{0,1:T(8,128)(2,1)S(1)} %bitcast.91), kind=kLoop, calls=%fused_computation.13 | loop fusion | flops 37748736 | bytes 16777216 | tf_op jit(solution)/shard_map/transpose(jvp(jit(silu)))/add_any | solution.py:23
  182.5 1.9 copy-done.9
  184.4 3.7 %fusion.30 = bf16[512,2048]{0,1:T(8,128)(2,1)} fusion(bf16[1024,512]{1,0:T(8,128)(2,1)S(1)} %copy-done.12, bf16[1024,2048]{0,1:T(8,128)(2,1)S(1)} %fusion.3), kind=kOutput, calls=%fused_computation.97 | convolution fusion | flops 2147483648 | bytes 7340032 | tf_op jit(solution)/shard_map/transpose(jvp())/dot_general | solution.py:24
  188.2 4.9 %fusion.9 = (f32[1024]{0:T(1024)S(1)}, bf16[1024,512]{1,0:T(8,128)(2,1)S(1)}) fusion(bf16[32,32,512]{2,1,0:T(8,128)(2,1)S(1)} %copy-done.4, f32[1024]{0:T(1024)S(1)} %copy-done.16, bf16[1024,2048]{0,1:T(8,128)(2,1)} %copy-done.9, bf16[512,2048]{1,0:T(8,128)(2,1)S(1)} %copy-done), kind=kOutput, calls=%fused_computation.30 | convolution fusion | flops 2150104064 | bytes 8396800 | tf_op jit(solution)/shard_map/transpose(jvp())/dot_general | solution.py:24
  194.2 2.8 fusion.13
  197.0 7.3 %all-to-all-start.2 = ((bf16[32,32,512]{2,1,0:T(8,128)(2,1)}), bf16[32,32,512]{2,1,0:T(8,128)(2,1)S(1)}, u32[]{:S(2)}, u32[]{:S(2)}) async-start(bf16[32,32,512]{2,1,0:T(8,128)(2,1)} %bitcast.99), calls=%async_computation.2 | async-start | bytes 2097152 | tf_op jit(solution)/shard_map/all_to_all | solution.py:86
  204.4 50.9 %reduce-scatter.5.cloned.1.call-done = bf16[512,16]{0,1:T(8,128)(2,1)} async-done(((bf16[512,512]{0,1:T(8,128)(2,1)}), bf16[512,16]{0,1:T(8,128)(2,1)}) %reduce-scatter.5.cloned.1.call-update) | async-done | bytes 16400 | tf_op jit(solution)/shard_map/reduce_scatter | solution.py:94
  255.3 17.5 %psum.7 = bf16[512,16]{0,1:T(8,128)(2,1)S(1)} all-reduce(bf16[512,16]{0,1:T(8,128)(2,1)} %reduce-scatter.5.cloned.1.call-done), channel_id=1, replica_groups=mesh['dp'=32,'rep'=4] {'rep'}, use_global_device_ids=true, to_apply=%region_16.17 | all-reduce | flops 8192 | bytes 32768 | tf_op jit(solution)/shard_map/psum | solution.py:100
  273.4 2.6 gather_fusion.1
  276.0 2.0 broadcast_select_fusion
  278.0 59.2 %reduce-scatter.3.cloned.1.call-done = bf16[512,64]{0,1:T(8,128)(2,1)} async-done(((bf16[512,2048]{0,1:T(8,128)(2,1)}), bf16[512,64]{0,1:T(8,128)(2,1)}) %reduce-scatter.3.cloned.1.call-update) | async-done | bytes 65552 | tf_op jit(solution)/shard_map/reduce_scatter | solution.py:91
  337.2 12.9 %all-gather = bf16[2048,64]{0,1:T(8,128)(2,1)S(1)} all-gather(bf16[512,64]{0,1:T(8,128)(2,1)} %reduce-scatter.3.cloned.1.call-done), channel_id=2, replica_groups=mesh['dp'=32,'rep'=4] {'rep'}, dimensions={0}, use_global_device_ids=true | all-gather | bytes 327680 | tf_op jit(solution)/shard_map/all_gather | solution.py:99
  (85 shorter events, 8.3 us)
Async XLA Ops:
  7.2 65.4 %copy-start = (bf16[512,2048]{1,0:T(8,128)(2,1)S(1)}, bf16[512,2048]{1,0:T(8,128)(2,1)}, u32[]{:S(2)}) copy-start(bf16[512,2048]{1,0:T(8,128)(2,1)} %param.9) | copy-start | bytes 6291460
  7.2 47.9 %copy-start.1 = (s32[1,512]{1,0:T(1,128)S(1)}, s32[1,512]{1,0:T(1,128)}, u32[]{:S(2)}) copy-start(s32[1,512]{1,0:T(1,128)} %param.13) | copy-start | bytes 6148
  8.0 54.0 %copy-start.21 = (s32[512,1]{0,1:T(1,128)}, s32[512,1]{0,1:T(1,128)S(1)}, u32[]{:S(2)}) copy-start(s32[512,1]{0,1:T(1,128)S(1)} %compare_select_fusion.1) | copy-start | bytes 6148
  12.0 53.0 %all-to-all-start.1 = ((bf16[32,32,512]{2,1,0:T(8,128)(2,1)}), bf16[32,32,512]{2,1,0:T(8,128)(2,1)S(1)}, u32[]{:S(2)}, u32[]{:S(2)}) async-start(bf16[32,32,512]{2,1,0:T(8,128)(2,1)} %bitcast.97), calls=%async_computation.1 | async-start | bytes 2097152 | tf_op jit(solution)/shard_map/all_to_all | solution.py:62
  65.0 13.3 %copy-start.3 = (bf16[32,32,512]{2,1,0:T(8,128)(2,1)}, bf16[32,32,512]{2,1,0:T(8,128)(2,1)S(1)}, u32[]{:S(2)}) copy-start(bf16[32,32,512]{2,1,0:T(8,128)(2,1)S(1)} %all-to-all-done.1) | copy-start | bytes 3145732
  65.0 53.0 %all-to-all-start = ((bf16[32,32,512]{2,1,0:T(8,128)(2,1)}), bf16[32,32,512]{2,1,0:T(8,128)(2,1)}, u32[]{:S(2)}, u32[]{:S(2)}) async-start(bf16[32,32,512]{2,1,0:T(8,128)(2,1)} %bitcast.98), calls=%async_computation | async-start | bytes 2097152 | tf_op jit(solution)/shard_map/all_to_all | solution.py:63
  70.9 184.3 %reduce-scatter.5.cloned.1.call-start = ((), (), s32[]{:S(2)}) async-start(), calls=%async_computation.6 | async-start | bytes 540672 | tf_op jit(solution)/shard_map/reduce_scatter | solution.py:94
  71.6 6.7 %copy-start.15 = (f32[1024]{0:T(1024)}, f32[1024]{0:T(1024)S(1)}, u32[]{:S(2)}) copy-start(f32[1024]{0:T(1024)S(1)} %div.65) | copy-start | bytes 12292
  72.2 6.1 %copy-start.19 = (f32[1024]{0:T(1024)}, f32[1024]{0:T(1024)S(1)}, u32[]{:S(2)}) copy-start(f32[1024]{0:T(1024)S(1)} %add.151) | copy-start | bytes 12292
  72.2 6.1 %copy-start.17 = (f32[1024]{0:T(1024)}, f32[1024]{0:T(1024)S(1)}, u32[]{:S(2)}) copy-start(f32[1024]{0:T(1024)S(1)} %rsqrt.20) | copy-start | bytes 12292
  72.6 5.7 %copy-start.11 = (bf16[1024,512]{1,0:T(8,128)(2,1)}, bf16[1024,512]{1,0:T(8,128)(2,1)S(1)}, u32[]{:S(2)}) copy-start(bf16[1024,512]{1,0:T(8,128)(2,1)S(1)} %multiply_convert_fusion.2) | copy-start | bytes 3145732
  78.3 1.9 copy-start.5
  82.0 21.5 %copy-start.6 = (bf16[1024,512]{0,1:T(8,128)(2,1)}, bf16[1024,512]{0,1:T(8,128)(2,1)S(1)}, u32[]{:S(2)}) copy-start(bf16[1024,512]{0,1:T(8,128)(2,1)S(1)} %get-tuple-element.10) | copy-start | bytes 3145732
  103.5 14.5 %copy-start.14 = (bf16[512,512]{1,0:T(8,128)(2,1)S(1)}, bf16[512,512]{1,0:T(8,128)(2,1)}, u32[]{:S(2)}) copy-start(bf16[512,512]{1,0:T(8,128)(2,1)} %param.10) | copy-start | bytes 1572868
  118.0 10.1 %copy-start.2 = (bf16[8,1024,1024]{2,1,0:T(8,128)(2,1)S(1)}, bf16[8,1024,1024]{2,1,0:T(8,128)(2,1)}, u32[]{:S(2)}) copy-start(bf16[8,1024,1024]{2,1,0:T(8,128)(2,1)} %get-tuple-element.17) | copy-start | bytes 50331652
  128.1 4.0 %copy-start.8 = (f32[1024,1024]{1,0:T(8,128)S(1)}, f32[1024,1024]{1,0:T(8,128)}, u32[]{:S(2)}) copy-start(f32[1024,1024]{1,0:T(8,128)} %fusion.6) | copy-start | bytes 12582916
  128.2 4.0 %copy-start.10 = (bf16[1024,512]{0,1:T(8,128)(2,1)S(1)}, bf16[1024,512]{0,1:T(8,128)(2,1)}, u32[]{:S(2)}) copy-start(bf16[1024,512]{0,1:T(8,128)(2,1)} %get-tuple-element.11) | copy-start | bytes 3145732
  132.2 23.7 %copy-start.13 = (bf16[1024,512]{0,1:T(8,128)(2,1)S(1)}, bf16[1024,512]{0,1:T(8,128)(2,1)}, u32[]{:S(2)}) copy-start(bf16[1024,512]{0,1:T(8,128)(2,1)} %get-tuple-element.9) | copy-start | bytes 3145732
  155.9 9.9 %copy-start.7 = (bf16[1024,512]{0,1:T(8,128)(2,1)S(1)}, bf16[1024,512]{0,1:T(8,128)(2,1)}, u32[]{:S(2)}) copy-start(bf16[1024,512]{0,1:T(8,128)(2,1)} %copy-done.6) | copy-start | bytes 3145732
  176.1 161.1 %reduce-scatter.3.cloned.1.call-start = ((), (), s32[]{:S(2)}) async-start(), calls=%async_computation.5 | async-start | bytes 2162688 | tf_op jit(solution)/shard_map/reduce_scatter | solution.py:91
  176.1 8.3 %copy-start.12 = (bf16[1024,512]{1,0:T(8,128)(2,1)S(1)}, bf16[1024,512]{1,0:T(8,128)(2,1)}, u32[]{:S(2)}) copy-start(bf16[1024,512]{1,0:T(8,128)(2,1)} %copy-done.11) | copy-start | bytes 3145732
  182.5 1.9 copy-start.9
  184.4 3.7 %copy-start.4 = (bf16[32,32,512]{2,1,0:T(8,128)(2,1)S(1)}, bf16[32,32,512]{2,1,0:T(8,128)(2,1)}, u32[]{:S(2)}) copy-start(bf16[32,32,512]{2,1,0:T(8,128)(2,1)} %copy-done.3) | copy-start | bytes 3145732
  184.4 3.7 %copy-start.16 = (f32[1024]{0:T(1024)S(1)}, f32[1024]{0:T(1024)}, u32[]{:S(2)}) copy-start(f32[1024]{0:T(1024)} %copy-done.15) | copy-start | bytes 12292
  188.2 4.9 %copy-start.20 = (f32[1024]{0:T(1024)S(1)}, f32[1024]{0:T(1024)}, u32[]{:S(2)}) copy-start(f32[1024]{0:T(1024)} %copy-done.19) | copy-start | bytes 12292
  188.2 4.9 %copy-start.18 = (f32[1024]{0:T(1024)S(1)}, f32[1024]{0:T(1024)}, u32[]{:S(2)}) copy-start(f32[1024]{0:T(1024)} %copy-done.17) | copy-start | bytes 12292
  193.1 11.2 %copy-start.22 = (s32[512,1]{0,1:T(1,128)S(1)}, s32[512,1]{0,1:T(1,128)}, u32[]{:S(2)}) copy-start(s32[512,1]{0,1:T(1,128)} %copy-done.21) | copy-start | bytes 6148
  193.1 11.2 %copy-start.23 = (s32[1,512]{1,0:T(1,128)S(1)}, s32[1,512]{1,0:T(1,128)}, u32[]{:S(2)}) copy-start(s32[1,512]{1,0:T(1,128)} %param.11) | copy-start | bytes 6148
  197.0 76.4 %all-to-all-start.2 = ((bf16[32,32,512]{2,1,0:T(8,128)(2,1)}), bf16[32,32,512]{2,1,0:T(8,128)(2,1)S(1)}, u32[]{:S(2)}, u32[]{:S(2)}) async-start(bf16[32,32,512]{2,1,0:T(8,128)(2,1)} %bitcast.99), calls=%async_computation.2 | async-start | bytes 2097152 | tf_op jit(solution)/shard_map/all_to_all | solution.py:86
Sparse Core Ops, SparseCore 0:
  176.2 79.0 reduce-scatter.4
  258.8 78.2 reduce-scatter.2
